TPU v7x, 32 devices: a whole 2x2x4 slice. The times are simulated.
32 devices in a mesh: tower: 4 (over y, x), rank: 8 (over z, core).
Axes of the slice: x: 2, y: 2, z: 4, core: 2. Of those that a mesh axis runs over, the one named last changes fastest.
Arguments:
- pooled: bfloat16 [2, 2048, 1024], P(None, ('tower', 'rank')), may hold values from -8 to 8
- feature_order: int32 [4, 4], P('tower'), may hold values from 0 to 3, as said below
- cross_weight: bfloat16 [4, 3, 512, 512], P('tower'), may hold values from -0.25 to 0.25
- cross_bias: float32 [4, 3, 512], P('tower'), may hold values from -3 to 3
- compress_weight: bfloat16 [4, 128, 512], P('tower'), may hold values from -0.25 to 0.25
- norm_gain: float32 [4, 128], P('tower'), may hold values from 0.1 to 1.9
- mlp_weight: bfloat16 [4096, 512], P(('tower', 'rank')), may hold values from -0.25 to 0.25
- mlp_bias: bfloat16 [4096], P(('tower', 'rank')), may hold values from -3 to 3
- out_weight: bfloat16 [4096], P(('tower', 'rank')), may hold values from -0.09375 to 0.09375
Outputs:
- logits: float32 [2, 8, 128], P(None, 'rank', 'tower')
Inputs may be any that keep to these rules, and one draw needn't show every extreme that they name: `feature_order`: each row is an ordering of 0 to 3.
All inputs are finite; a program needn't handle non-finite values.
Results may differ from a plain program's by a relative error of at most 0.0076.
Values may be sent and summed in bfloat16 or wider, within the bound.
A program may use at most 64 MiB of HBM per device.

v0:
```python
import functools

import jax
import jax.numpy as jnp
from jax import lax
from jax.experimental import pallas as pl
from jax.experimental.pallas import tpu as pltpu
from jax.sharding import PartitionSpec as P

E = 128
CD = 128
CORES = 2

epsilon = 1e-06
MESH = pl.DeviceIdType.MESH


def fused(
    n_tower,
    n_rank,
    order,
    pooled,
    cross_w,
    cross_b,
    compress,
    gain,
    mlp_w,
    hid_b,
    hid_o,
    out,
    arrived,
    weights,
    compress_v,
    bias_v,
    flat_v,
    gain_v,
    bias_c,
    gain_c,
    first,
    state_a,
    state_b,
    towers,
    mixed,
    rows,
    packs_b,
    packs_o,
    flat_b,
    flat_o,
    hid_c,
    parts,
    load_sem,
    a2a_send,
    a2a_recv,
    row_send,
    row_recv,
    mate_send,
    mate_recv,
    pack_send,
    pack_recv,
    tower_send,
    tower_recv,
    part_send,
    part_recv,
):
    micro = pooled.shape[0]
    block = arrived[0].shape[-1]
    layers, td = cross_w.shape[1], cross_w.shape[2]
    smalls = ((hid_b, packs_b), (hid_o, packs_o))
    chips = n_rank // CORES
    t = lax.axis_index("tower")
    r = lax.axis_index("rank")
    z = r // CORES
    c = lax.rem(r, CORES)
    mate = z * CORES + (1 - c)

    loads = [
        pltpu.make_async_copy(cross_b, bias_v, load_sem.at[1]),
        pltpu.make_async_copy(gain, gain_v, load_sem.at[2]),
        pltpu.make_async_copy(hid_b, packs_b.at[r], load_sem.at[3]),
        pltpu.make_async_copy(hid_o, packs_o.at[r], load_sem.at[4]),
        pltpu.make_async_copy(compress.at[0], compress_v, load_sem.at[5]),
        pltpu.make_async_copy(mlp_w, rows.at[r], load_sem.at[6]),
    ]
    for b in range(micro):
        own = pooled.at[b, :, pl.ds(pl.multiple_of(r * block, block), block)]
        loads.append(pltpu.make_async_copy(own, arrived[b].at[r], load_sem.at[7 + layers + b]))
    w_loads = [pltpu.make_async_copy(cross_w.at[0, l], weights.at[l], load_sem.at[7 + l]) for l in range(layers)]

    barrier = pltpu.get_barrier_semaphore()
    for d in range(1, n_rank):
        pl.semaphore_signal(barrier, inc=1, device_id={"rank": lax.rem(r + d, n_rank)}, device_id_type=MESH)
    for d in range(1, n_tower):
        pl.semaphore_signal(barrier, inc=1, device_id={"tower": lax.rem(t + d, n_tower)}, device_id_type=MESH)
    for copy in loads + w_loads:
        copy.start()
    pl.semaphore_wait(barrier, n_rank + n_tower - 2)

    def spread(b, source, target, src_ref):
        return pltpu.make_async_remote_copy(
            src_ref=src_ref,
            dst_ref=arrived[b].at[source],
            send_sem=a2a_send.at[b, target],
            recv_sem=a2a_recv.at[b, source],
            device_id={"rank": target},
            device_id_type=MESH,
        )

    def chip_at(k):
        return lax.rem(z + k + chips, chips)

    others = [
        chip_at(k) * CORES + (c if twin == 0 else 1 - c)
        for k in sorted(range(chips), key=lambda k: -min(k, chips - k))
        for twin in range(CORES)
        if (k, twin) != (0, 0)
    ]
    a2a = []
    for b in range(micro):
        for peer in others:
            columns = pl.ds(pl.multiple_of(peer * block, block), block)
            copy = spread(b, r, peer, pooled.at[b, :, columns])
            copy.start()
            a2a.append(copy)

    half = rows.shape[1] // 2
    seen = set()

    def piece(k, h):
        return rows.at[chip_at(k) * CORES + c, pl.ds(h * half, half)]

    def row_copy(k, h, way, src_ref):
        return pltpu.make_async_remote_copy(
            src_ref=src_ref,
            dst_ref=piece(k, h),
            send_sem=row_send.at[abs(k), h, max(way, 0)],
            recv_sem=row_recv.at[chip_at(k), h],
            device_id={"rank": chip_at(way) * CORES + c},
            device_id_type=MESH,
        )

    def arrive(k, h):
        if k % chips and (k % chips, h) not in seen:
            seen.add((k % chips, h))
            row_copy(k, h, 1, piece(k, h)).wait_recv()

    row_sends = []

    def hop(s):
        for h, way in ((0, 1), (1, -1), (1, 1), (0, -1)):
            reach = chips // 2 if (h, way) in ((0, 1), (1, -1)) else (chips - 1) // 2
            if s < reach:
                k = -way * s
                if s:
                    arrive(k, h)
                copy = row_copy(k, h, way, piece(k, h) if s else mlp_w.at[pl.ds(h * half, half)])
                copy.start()
                row_sends.append(copy)

    def mate_copy(k, src_ref):
        return pltpu.make_async_remote_copy(
            src_ref=src_ref,
            dst_ref=rows.at[chip_at(k) * CORES + c],
            send_sem=mate_send.at[k],
            recv_sem=mate_recv.at[k],
            device_id={"rank": mate},
            device_id_type=MESH,
        )

    def share(k):
        for h in range(2):
            arrive(k, h)
        copy = mate_copy(k, rows.at[chip_at(k) * CORES + c] if k else mlp_w)
        copy.start()
        row_sends.append(copy)

    packing = []
    for d in range(1, n_rank):
        for i, (source, target) in enumerate(smalls):
            copy = pltpu.make_async_remote_copy(
                src_ref=source,
                dst_ref=target.at[r],
                send_sem=pack_send.at[i, d - 1],
                recv_sem=pack_recv.at[i, d - 1],
                device_id={"rank": lax.rem(r + d, n_rank)},
                device_id_type=MESH,
            )
            copy.start()
            packing.append(copy)

    hop(0)
    share(0)
    near = [k for k in range(1, chips) if min(k, chips - k) == 1]
    far = [k for k in sorted(range(1, chips), key=lambda k: min(k, chips - k)) if k not in near]

    for copy in loads:
        copy.wait()
    for l in range(layers):
        flat_v[l : l + 1, :] = bias_v[l]
    bias_c[...] = flat_v[...].T
    gain_c[...] = jnp.broadcast_to(gain_v[...], (8, CD)).T

    per_feature = n_rank // order.shape[1]
    height = arrived[0].shape[1]
    exchange = []
    for b in range(micro):
        cols = slice(b * block, (b + 1) * block)
        for peer in others:
            spread(b, peer, r, arrived[b].at[peer]).wait_recv()
        for slot in range(order.shape[1]):
            feature = order[0, slot]
            for h in range(per_feature):
                first[slot * E + h * height : slot * E + (h + 1) * height, cols] = arrived[b][
                    feature * per_feature + h
                ]

        current, spare = first, state_a
        for l in range(layers):
            if b == 0:
                w_loads[l].wait()
            for m in range(0, td, E):
                here = slice(m, m + E)
                product = (
                    jnp.dot(weights[l, here, :], current[:, cols], preferred_element_type=jnp.float32)
                    + bias_c[here, l : l + 1]
                )
                spare[here, cols] = (
                    first[here, cols].astype(jnp.float32) * product
                    + current[here, cols].astype(jnp.float32)
                ).astype(jnp.bfloat16)
            current, spare = spare, (state_b if spare is state_a else state_a)
        squeezed = jnp.dot(compress_v[...], current[:, cols], preferred_element_type=jnp.float32)
        inverse_rms = lax.rsqrt(jnp.mean(squeezed * squeezed, axis=0, keepdims=True) + epsilon)
        towers[b][t] = (squeezed * inverse_rms * gain_c[:, 0:1]).astype(jnp.bfloat16)

        for d in range(1, n_tower):
            copy = pltpu.make_async_remote_copy(
                src_ref=towers[b].at[t],
                dst_ref=towers[b].at[t],
                send_sem=tower_send.at[b, d - 1],
                recv_sem=tower_recv.at[b, d - 1],
                device_id={"tower": lax.rem(t + d, n_tower)},
                device_id_type=MESH,
            )
            copy.start()
            exchange.append(copy)

    hop(1)
    for k in near:
        share(k)
    for step in range(2, chips // 2):
        hop(step)
    for copy in packing:
        copy.wait_recv()
    for s in range(n_rank):
        flat_b[s : s + 1, :] = packs_b[s].astype(jnp.float32)
        flat_o[s : s + 1, :] = packs_o[s].astype(jnp.float32)
    turned_b = flat_b[...].T
    turned_o = flat_o[...].T
    for s in range(n_rank):
        hid_c[s, 0] = turned_b[:, s : s + 1]
        hid_c[s, 1] = turned_o[:, s : s + 1]

    for b in range(micro):
        cols = slice(b * block, (b + 1) * block)
        for copy in exchange[b * (n_tower - 1) : (b + 1) * (n_tower - 1)]:
            copy.wait_recv()
        values = [towers[b][u].astype(jnp.float32) for u in range(n_tower)]
        gram = {}
        for u in range(n_tower):
            for v in range(u, n_tower):
                gram[u, v] = gram[v, u] = jnp.sum(values[u] * values[v], axis=0, keepdims=True) / CD
        for u in range(n_tower):
            total = values[u]
            for v in range(n_tower):
                total = total + gram[u, v] * values[v]
            mixed[u * CD : (u + 1) * CD, cols] = total.astype(jnp.bfloat16)

    score = jnp.zeros((rows.shape[1], mixed.shape[1]), jnp.float32)

    def add(s, score):
        hidden = jnp.dot(rows[s], mixed[...], preferred_element_type=jnp.float32) + hid_c[s, 0]
        return score + jnp.maximum(hidden, 0.0) * hid_c[s, 1]

    def add_mate(k, score):
        s = chip_at(k) * CORES + 1 - c
        pltpu.make_async_remote_copy(
            src_ref=rows.at[s],
            dst_ref=rows.at[s],
            send_sem=mate_send.at[k],
            recv_sem=mate_recv.at[k],
            device_id={"rank": mate},
            device_id_type=MESH,
        ).wait_recv()
        return add(s, score)

    for k in [0] + near:
        score = add(chip_at(k) * CORES + c, score)
    for k in [0] + near:
        score = add_mate(k, score)
    for k in far:
        share(k)
        score = add(chip_at(k) * CORES + c, score)
    for k in far:
        score = add_mate(k, score)
    parts[t] = jnp.sum(score, axis=0, keepdims=True)

    sums = []
    for d in range(1, n_tower):
        copy = pltpu.make_async_remote_copy(
            src_ref=parts.at[t],
            dst_ref=parts.at[t],
            send_sem=part_send.at[d - 1],
            recv_sem=part_recv.at[d - 1],
            device_id={"tower": lax.rem(t + d, n_tower)},
            device_id_type=MESH,
        )
        copy.start()
        sums.append(copy)

    for copy in a2a + packing + exchange + row_sends:
        copy.wait_send()
    for copy in sums:
        copy.wait_recv()
    logits = parts[0]
    for u in range(1, n_tower):
        logits = logits + parts[u]
    width = block // n_tower
    for u in range(n_tower):

        @pl.when(t == u)
        def _():
            for b in range(micro):
                out[b] = logits[:, b * block + u * width : b * block + (u + 1) * width]

    for copy in sums:
        copy.wait_send()


def in_one_kernel(
    n_tower, n_rank, pooled, order, cross_w, cross_b, compress, gain, mlp_w, mlp_bias, out_weight
):
    micro, height, samples = pooled.shape
    block = samples // n_rank
    _, layers, td, _ = cross_w.shape
    hid, width = mlp_w.shape
    chips = n_rank // CORES
    every = micro * block
    bf16, f32 = jnp.bfloat16, jnp.float32
    dma = pltpu.SemaphoreType.DMA
    hbm = pl.BlockSpec(memory_space=pl.ANY)
    return pl.pallas_call(
        functools.partial(fused, n_tower, n_rank),
        out_shape=jax.ShapeDtypeStruct((micro, 1, block // n_tower), f32),
        in_specs=[pl.BlockSpec(memory_space=pltpu.SMEM)] + [hbm] * 8,
        out_specs=pl.BlockSpec(memory_space=pltpu.VMEM),
        scratch_shapes=[
            [pltpu.VMEM((n_rank, height, block), bf16)] * micro,
            pltpu.VMEM((layers, td, td), bf16),
            pltpu.VMEM((CD, td), bf16),
            pltpu.VMEM((layers, 1, td), f32),
            pltpu.VMEM((8, td), f32),
            pltpu.VMEM((1, CD), f32),
            pltpu.VMEM((td, 8), f32),
            pltpu.VMEM((CD, 8), f32),
            pltpu.VMEM((td, every), bf16),
            pltpu.VMEM((td, every), bf16),
            pltpu.VMEM((td, every), bf16),
            [pltpu.VMEM((n_tower, CD, block), bf16)] * micro,
            pltpu.VMEM((width, every), bf16),
            pltpu.VMEM((n_rank, hid, width), bf16),
            pltpu.VMEM((n_rank, 1, hid), bf16),
            pltpu.VMEM((n_rank, 1, hid), bf16),
            pltpu.VMEM((n_rank, hid), f32),
            pltpu.VMEM((n_rank, hid), f32),
            pltpu.VMEM((n_rank, 2, hid, 1), f32),
            pltpu.VMEM((n_tower, 1, every), f32),
            dma((7 + layers + micro,)),
            dma((micro, n_rank)),
            dma((micro, n_rank)),
            dma((chips, 2, 2)),
            dma((chips, 2)),
            dma((chips,)),
            dma((chips,)),
            dma((2, n_rank - 1)),
            dma((2, n_rank - 1)),
            dma((micro, n_tower - 1)),
            dma((micro, n_tower - 1)),
            dma((n_tower - 1,)),
            dma((n_tower - 1,)),
        ],
        compiler_params=pltpu.CompilerParams(collective_id=0, has_side_effects=True),
    )(
        order,
        pooled,
        cross_w,
        cross_b.swapaxes(0, 1),
        compress,
        gain,
        mlp_w,
        mlp_bias[None],
        out_weight[None],
    )


def tower_block(first, weights, biases, compress, gain):
    first_f = first.astype(jnp.float32)
    current = first
    for layer in range(weights.shape[0]):
        product = (
            jnp.dot(weights[layer], current, preferred_element_type=jnp.float32)
            + biases[layer][:, None]
        )
        current = (first_f * product + current.astype(jnp.float32)).astype(jnp.bfloat16)
    squeezed = jnp.dot(compress, current, preferred_element_type=jnp.float32)
    inverse_rms = lax.rsqrt(jnp.mean(squeezed * squeezed, axis=0, keepdims=True) + epsilon)
    return (squeezed * inverse_rms * gain[:, None]).astype(jnp.bfloat16)


def interact(joined):
    samples_now = joined.shape[1]
    values_f = joined.astype(jnp.float32).reshape(-1, CD, samples_now)
    gram = jnp.einsum("tck,uck->tuk", values_f, values_f, precision=lax.Precision.HIGHEST) / CD
    mixed = values_f + jnp.einsum("tuk,uck->tck", gram, values_f, precision=lax.Precision.HIGHEST)
    return mixed.reshape(-1, samples_now).astype(jnp.bfloat16)


def logit_terms(hidden_rows, hidden_bias, hidden_out, features):
    hidden = (
        jnp.dot(hidden_rows, features, preferred_element_type=jnp.float32)
        + hidden_bias.astype(jnp.float32)[:, None]
    )
    return jnp.sum(
        jax.nn.relu(hidden) * hidden_out.astype(jnp.float32)[:, None], axis=0, keepdims=True
    )


def by_collectives(
    pooled,
    feature_order,
    cross_weight,
    cross_bias,
    compress_weight,
    norm_gain,
    mlp_weight,
    mlp_bias,
    out_weight,
):
    micro_count = pooled.shape[0]
    arriving = [
        lax.all_to_all(pooled[batch], "rank", split_axis=1, concat_axis=0, tiled=True)
        for batch in range(micro_count)
    ]
    hidden_rows, hidden_bias, hidden_out = (
        lax.all_gather(mlp_weight, "rank", axis=0, tiled=True),
        lax.all_gather(mlp_bias, "rank", axis=0, tiled=True),
        lax.all_gather(out_weight, "rank", axis=0, tiled=True),
    )
    results = []
    for batch in range(micro_count):
        arrived = arriving[batch]
        samples_here = arrived.shape[1]
        first = jnp.take(arrived.reshape(-1, E, samples_here), feature_order[0], axis=0).reshape(
            -1, samples_here
        )
        compressed = tower_block(
            first, cross_weight[0], cross_bias[0], compress_weight[0], norm_gain[0]
        )
        all_towers = lax.all_gather(compressed, "tower", axis=0, tiled=True)
        partial_value = logit_terms(hidden_rows, hidden_bias, hidden_out, interact(all_towers))
        logit_row = lax.psum_scatter(partial_value, "tower", scatter_dimension=1, tiled=True)
        results.append(logit_row)
    return jnp.stack(results)


def fits(mesh, pooled, mlp_w):
    height, hid = pooled.shape[1], mlp_w.shape[0]
    return mesh.shape["rank"] % CORES == 0 and E % height == 0 and height % 16 == 0 and hid % 128 == 0


def solution(mesh):
    def on_device(*args):
        if fits(mesh, args[0], args[6]):
            return in_one_kernel(mesh.shape["tower"], mesh.shape["rank"], *args)
        return by_collectives(*args)

    return jax.shard_map(
        on_device,
        mesh=mesh,
        in_specs=(
            P(None, ("tower", "rank"), None),
            P("tower", None),
            P("tower", None, None, None),
            P("tower", None, None),
            P("tower", None, None),
            P("tower", None),
            P(("tower", "rank"), None),
            P(("tower", "rank")),
            P(("tower", "rank")),
        ),
        out_specs=P(None, "rank", "tower"),
        check_vma=False,
    )
```

profile of v0, /device:TPU:0, one launch (start us, length us, event | category | flops | bytes accessed | tf_op | source)
XLA Modules:
  0.0 28.4 jit_solution(11411246637161638174)
XLA Ops:
  0.0 27.1 %shard_map.91 = f32[2,1,32]{2,1,0:T(1,128)} custom-call(s32[1,4]{1,0:T(1,128)} %order.1, bf16[2,64,1024]{2,1,0:T(8,128)(2,1)} %pooled.1, bf16[1,3,512,512]{3,2,1,0:T(8,128)(2,1)} %cross_w.1, f32[3,1,512]{2,1,0:T(1,128)} %bitcast.3, bf16[1,128,512]{2,1,0:T(8,128)(2,1)} %compress.1, f32[1,128]{1,0:T(1,128)} %gain.1, bf16[128,512]{1,0:T(8,128)(2,1)} %mlp_w.1, ...), custom_call_target="tpu_custom_call" | custom-call | tf_op jit(solution)/shard_map/pallas_call | solution.py:351
  27.1 1.2 %copy.11 = f32[2,1,32]{2,1,0:T(1,128)} copy(f32[2,1,32]{2,1,0:T(1,128)} %shard_map.91) | data formatting | bytes 512
where the time goes:
time: 28.5 us; the launch traced here: 28.4 us
  Pallas kernels  27.1 us (95%)
  local copies, waits for them, and re-layouts  1.24 us (4%)
    pallas_call x1, Pallas kernels, in_one_kernel(): pl.pallas_call(functools.partial(fused, n_tower, n_rank), out_shape=jax.S...  27.1 us
    unnamed x1, local copies, waits for them, and re-layouts  1.24 us

commit v1 on v0

--- a/solution.py
+++ b/solution.py
@@ -15,10 +15,14 @@
 MESH = pl.DeviceIdType.MESH
 
 
+def drain(ref, sem):
+    pltpu.make_async_copy(ref, ref, sem).wait()
+
+
 def fused(
     n_tower,
     n_rank,
-    order,
+    order_any,
     pooled,
     cross_w,
     cross_b,
@@ -28,6 +32,7 @@
     hid_b,
     hid_o,
     out,
+    order,
     arrived,
     weights,
     compress_v,
@@ -53,7 +58,6 @@
     a2a_recv,
     row_send,
     row_recv,
-    mate_send,
     mate_recv,
     pack_send,
     pack_recv,
@@ -74,24 +78,26 @@
     mate = z * CORES + (1 - c)
 
     loads = [
-        pltpu.make_async_copy(cross_b, bias_v, load_sem.at[1]),
-        pltpu.make_async_copy(gain, gain_v, load_sem.at[2]),
-        pltpu.make_async_copy(hid_b, packs_b.at[r], load_sem.at[3]),
-        pltpu.make_async_copy(hid_o, packs_o.at[r], load_sem.at[4]),
-        pltpu.make_async_copy(compress.at[0], compress_v, load_sem.at[5]),
-        pltpu.make_async_copy(mlp_w, rows.at[r], load_sem.at[6]),
+        pltpu.make_async_copy(cross_b, bias_v, load_sem.at[0]),
+        pltpu.make_async_copy(gain, gain_v, load_sem.at[0]),
+        pltpu.make_async_copy(hid_b, packs_b.at[r], load_sem.at[0]),
+        pltpu.make_async_copy(hid_o, packs_o.at[r], load_sem.at[0]),
+        pltpu.make_async_copy(compress.at[0], compress_v, load_sem.at[0]),
+        pltpu.make_async_copy(mlp_w, rows.at[r], load_sem.at[0]),
+        pltpu.make_async_copy(order_any, order, load_sem.at[0]),
     ]
+    own_loads = []
     for b in range(micro):
         own = pooled.at[b, :, pl.ds(pl.multiple_of(r * block, block), block)]
-        loads.append(pltpu.make_async_copy(own, arrived[b].at[r], load_sem.at[7 + layers + b]))
-    w_loads = [pltpu.make_async_copy(cross_w.at[0, l], weights.at[l], load_sem.at[7 + l]) for l in range(layers)]
+        own_loads.append(pltpu.make_async_copy(own, arrived[b].at[r], a2a_recv.at[b]))
+    w_loads = [pltpu.make_async_copy(cross_w.at[0, l], weights.at[l], load_sem.at[1 + l]) for l in range(layers)]
 
     barrier = pltpu.get_barrier_semaphore()
     for d in range(1, n_rank):
         pl.semaphore_signal(barrier, inc=1, device_id={"rank": lax.rem(r + d, n_rank)}, device_id_type=MESH)
     for d in range(1, n_tower):
         pl.semaphore_signal(barrier, inc=1, device_id={"tower": lax.rem(t + d, n_tower)}, device_id_type=MESH)
-    for copy in loads + w_loads:
+    for copy in own_loads + loads + w_loads:
         copy.start()
     pl.semaphore_wait(barrier, n_rank + n_tower - 2)
 
@@ -99,8 +105,8 @@
         return pltpu.make_async_remote_copy(
             src_ref=src_ref,
             dst_ref=arrived[b].at[source],
-            send_sem=a2a_send.at[b, target],
-            recv_sem=a2a_recv.at[b, source],
+            send_sem=a2a_send.at[b],
+            recv_sem=a2a_recv.at[b],
             device_id={"rank": target},
             device_id_type=MESH,
         )
@@ -114,13 +120,11 @@
         for twin in range(CORES)
         if (k, twin) != (0, 0)
     ]
-    a2a = []
     for b in range(micro):
         for peer in others:
             columns = pl.ds(pl.multiple_of(peer * block, block), block)
             copy = spread(b, r, peer, pooled.at[b, :, columns])
             copy.start()
-            a2a.append(copy)
 
     half = rows.shape[1] // 2
     seen = set()
@@ -132,7 +136,7 @@
         return pltpu.make_async_remote_copy(
             src_ref=src_ref,
             dst_ref=piece(k, h),
-            send_sem=row_send.at[abs(k), h, max(way, 0)],
+            send_sem=row_send.at[0],
             recv_sem=row_recv.at[chip_at(k), h],
             device_id={"rank": chip_at(way) * CORES + c},
             device_id_type=MESH,
@@ -160,7 +164,7 @@
         return pltpu.make_async_remote_copy(
             src_ref=src_ref,
             dst_ref=rows.at[chip_at(k) * CORES + c],
-            send_sem=mate_send.at[k],
+            send_sem=row_send.at[0],
             recv_sem=mate_recv.at[k],
             device_id={"rank": mate},
             device_id_type=MESH,
@@ -173,19 +177,17 @@
         copy.start()
         row_sends.append(copy)
 
-    packing = []
     for d in range(1, n_rank):
         for i, (source, target) in enumerate(smalls):
             copy = pltpu.make_async_remote_copy(
                 src_ref=source,
                 dst_ref=target.at[r],
-                send_sem=pack_send.at[i, d - 1],
-                recv_sem=pack_recv.at[i, d - 1],
+                send_sem=pack_send.at[i],
+                recv_sem=pack_recv.at[i],
                 device_id={"rank": lax.rem(r + d, n_rank)},
                 device_id_type=MESH,
             )
             copy.start()
-            packing.append(copy)
 
     hop(0)
     share(0)
@@ -201,11 +203,9 @@
 
     per_feature = n_rank // order.shape[1]
     height = arrived[0].shape[1]
-    exchange = []
     for b in range(micro):
         cols = slice(b * block, (b + 1) * block)
-        for peer in others:
-            spread(b, peer, r, arrived[b].at[peer]).wait_recv()
+        drain(arrived[b], a2a_recv.at[b])
         for slot in range(order.shape[1]):
             feature = order[0, slot]
             for h in range(per_feature):
@@ -236,21 +236,20 @@
             copy = pltpu.make_async_remote_copy(
                 src_ref=towers[b].at[t],
                 dst_ref=towers[b].at[t],
-                send_sem=tower_send.at[b, d - 1],
-                recv_sem=tower_recv.at[b, d - 1],
+                send_sem=tower_send.at[b],
+                recv_sem=tower_recv.at[b],
                 device_id={"tower": lax.rem(t + d, n_tower)},
                 device_id_type=MESH,
             )
             copy.start()
-            exchange.append(copy)
 
     hop(1)
     for k in near:
         share(k)
     for step in range(2, chips // 2):
         hop(step)
-    for copy in packing:
-        copy.wait_recv()
+    for i, (source, target) in enumerate(smalls):
+        drain(target.at[: n_rank - 1], pack_recv.at[i])
     for s in range(n_rank):
         flat_b[s : s + 1, :] = packs_b[s].astype(jnp.float32)
         flat_o[s : s + 1, :] = packs_o[s].astype(jnp.float32)
@@ -262,8 +261,7 @@
 
     for b in range(micro):
         cols = slice(b * block, (b + 1) * block)
-        for copy in exchange[b * (n_tower - 1) : (b + 1) * (n_tower - 1)]:
-            copy.wait_recv()
+        drain(towers[b].at[: n_tower - 1], tower_recv.at[b])
         values = [towers[b][u].astype(jnp.float32) for u in range(n_tower)]
         gram = {}
         for u in range(n_tower):
@@ -286,7 +284,7 @@
         pltpu.make_async_remote_copy(
             src_ref=rows.at[s],
             dst_ref=rows.at[s],
-            send_sem=mate_send.at[k],
+            send_sem=row_send.at[0],
             recv_sem=mate_recv.at[k],
             device_id={"rank": mate},
             device_id_type=MESH,
@@ -304,23 +302,25 @@
         score = add_mate(k, score)
     parts[t] = jnp.sum(score, axis=0, keepdims=True)
 
-    sums = []
     for d in range(1, n_tower):
         copy = pltpu.make_async_remote_copy(
             src_ref=parts.at[t],
             dst_ref=parts.at[t],
-            send_sem=part_send.at[d - 1],
-            recv_sem=part_recv.at[d - 1],
+            send_sem=part_send.at[0],
+            recv_sem=part_recv.at[0],
             device_id={"tower": lax.rem(t + d, n_tower)},
             device_id_type=MESH,
         )
         copy.start()
-        sums.append(copy)
-
-    for copy in a2a + packing + exchange + row_sends:
+
+    for b in range(micro):
+        drain(arrived[b].at[: n_rank - 1], a2a_send.at[b])
+        drain(towers[b].at[: n_tower - 1], tower_send.at[b])
+    for i, (source, target) in enumerate(smalls):
+        drain(target.at[: n_rank - 1], pack_send.at[i])
+    for copy in row_sends:
         copy.wait_send()
-    for copy in sums:
-        copy.wait_recv()
+    drain(parts.at[: n_tower - 1], part_recv.at[0])
     logits = parts[0]
     for u in range(1, n_tower):
         logits = logits + parts[u]
@@ -332,8 +332,7 @@
             for b in range(micro):
                 out[b] = logits[:, b * block + u * width : b * block + (u + 1) * width]
 
-    for copy in sums:
-        copy.wait_send()
+    drain(parts.at[: n_tower - 1], part_send.at[0])
 
 
 def in_one_kernel(
@@ -350,10 +349,11 @@
     hbm = pl.BlockSpec(memory_space=pl.ANY)
     return pl.pallas_call(
         functools.partial(fused, n_tower, n_rank),
-        out_shape=jax.ShapeDtypeStruct((micro, 1, block // n_tower), f32),
-        in_specs=[pl.BlockSpec(memory_space=pltpu.SMEM)] + [hbm] * 8,
+        out_shape=pltpu.VMEM((micro, 1, block // n_tower), f32),
+        in_specs=[hbm] * 9,
         out_specs=pl.BlockSpec(memory_space=pltpu.VMEM),
         scratch_shapes=[
+            pltpu.SMEM(order.shape, order.dtype),
             [pltpu.VMEM((n_rank, height, block), bf16)] * micro,
             pltpu.VMEM((layers, td, td), bf16),
             pltpu.VMEM((CD, td), bf16),
@@ -374,19 +374,18 @@
             pltpu.VMEM((n_rank, hid), f32),
             pltpu.VMEM((n_rank, 2, hid, 1), f32),
             pltpu.VMEM((n_tower, 1, every), f32),
-            dma((7 + layers + micro,)),
-            dma((micro, n_rank)),
-            dma((micro, n_rank)),
-            dma((chips, 2, 2)),
+            dma((1 + layers,)),
+            dma((micro,)),
+            dma((micro,)),
+            dma((1,)),
             dma((chips, 2)),
             dma((chips,)),
-            dma((chips,)),
-            dma((2, n_rank - 1)),
-            dma((2, n_rank - 1)),
-            dma((micro, n_tower - 1)),
-            dma((micro, n_tower - 1)),
-            dma((n_tower - 1,)),
-            dma((n_tower - 1,)),
+            dma((2,)),
+            dma((2,)),
+            dma((micro,)),
+            dma((micro,)),
+            dma((1,)),
+            dma((1,)),
         ],
         compiler_params=pltpu.CompilerParams(collective_id=0, has_side_effects=True),
     )(

time: 28.5 us -> 25.7 us (0.902)
  Pallas kernels: 27.1 us -> 25 us
  local copies, waits for them, and re-layouts: 1.24 us -> 0.56 us
    pallas_call x1, Pallas kernels: 27.1 us -> 25 us  [in_one_kernel(): pl.pallas_call(functools.partial(fused, n_tower, n_rank), out_shape=pltpu...]
    unnamed x1, local copies, waits for them, and re-layouts: 1.24 us -> 0.56 us
where the time goes in v1:
time: 25.7 us; the launch traced here: 25.5 us
  Pallas kernels  25 us (97%)
  local copies, waits for them, and re-layouts  0.56 us (2%)
    pallas_call x1, Pallas kernels, in_one_kernel(): pl.pallas_call(functools.partial(fused, n_tower, n_rank), out_shape=pltpu...  25 us
    unnamed x1, local copies, waits for them, and re-layouts  0.56 us

profile of v1, /device:TPU:0, one launch (start us, length us, event | category | flops | bytes accessed | tf_op | source)
XLA Modules:
  0.0 25.5 jit_solution(4904808528582974528)
XLA Ops:
  0.0 25.0 %shard_map.91 = f32[2,1,32]{2,1,0:T(1,128)S(1)} custom-call(s32[1,4]{1,0:T(1,128)} %order_any.1, bf16[2,64,1024]{2,1,0:T(8,128)(2,1)} %pooled.1, bf16[1,3,512,512]{3,2,1,0:T(8,128)(2,1)} %cross_w.1, f32[3,1,512]{2,1,0:T(1,128)} %bitcast.3, bf16[1,128,512]{2,1,0:T(8,128)(2,1)} %compress.1, f32[1,128]{1,0:T(1,128)} %gain.1, bf16[128,512]{1,0:T(8,128)(2,1)} %mlp_w.1, ...), custom_call_target="tpu_custom_call" | custom-call | tf_op jit(solution)/shard_map/pallas_call | solution.py:350
  25.0 0.6 %copy.11 = f32[2,1,32]{2,1,0:T(1,128)} copy(f32[2,1,32]{2,1,0:T(1,128)S(1)} %shard_map.91) | data formatting | bytes 512

commit v2 on v1

v2 whole, which is shorter than its diff:
```python
import functools

import jax
import jax.numpy as jnp
from jax import lax
from jax.experimental import pallas as pl
from jax.experimental.pallas import tpu as pltpu
from jax.sharding import PartitionSpec as P

E = 128
CD = 128
CORES = 2
LINE = 4
PIECES = 2

epsilon = 1e-06
MESH = pl.DeviceIdType.MESH


def drain(ref, sem):
    pltpu.make_async_copy(ref, ref, sem).wait()


def fused(
    n_tower,
    n_rank,
    order_any,
    pooled,
    cross_w,
    cross_b,
    compress,
    gain,
    mlp_w,
    hid_b,
    hid_o,
    out,
    order,
    arrived,
    weights,
    compress_v,
    bias_v,
    flat_v,
    gain_v,
    bias_c,
    gain_c,
    first,
    state_a,
    state_b,
    towers,
    mixed,
    rows,
    packs,
    flat,
    hid_c,
    score,
    parts,
    aside,
    diagonal,
    load_sem,
    a2a_send,
    a2a_recv,
    row_send,
    row_recv,
    pack_send,
    pack_recv,
    tower_send,
    tower_recv,
    mix_send,
    mix_recv,
    part_send,
    part_recv,
):
    micro = pooled.shape[0]
    block = arrived[0].shape[-1]
    layers, td = cross_w.shape[1], cross_w.shape[2]
    hid = mlp_w.shape[0]
    piece = hid // PIECES
    chunks = [(b, j) for b in range(micro) for j in range(CORES)]
    t = lax.axis_index("tower")
    r = lax.axis_index("rank")
    z = r // CORES
    c = lax.rem(r, CORES)
    mate = z * CORES + (1 - c)
    half = z // 2
    here, there = 1 + half, 2 - half
    inner = z == here
    outer = z != here
    steps = [1 << i for i in range(n_tower.bit_length() - 1)]

    barrier = pltpu.get_barrier_semaphore()

    def greet(**device):
        pl.semaphore_signal(barrier, inc=1, device_id=device, device_id_type=MESH)

    own_loads = [
        pltpu.make_async_copy(
            pooled.at[b, :, pl.ds(pl.multiple_of(((2 * half + c) * CORES + j) * block, block), block)],
            arrived[q].at[r],
            a2a_recv.at[q],
        )
        for q, (b, j) in enumerate(chunks)
    ]
    own_packs = [pltpu.make_async_copy(ref, packs.at[z, i], pack_recv.at[0]) for i, ref in enumerate((hid_b, hid_o))]
    loads = [
        pltpu.make_async_copy(cross_b, bias_v, load_sem.at[0]),
        pltpu.make_async_copy(gain, gain_v, load_sem.at[0]),
        pltpu.make_async_copy(compress.at[0], compress_v, load_sem.at[0]),
        pltpu.make_async_copy(mlp_w, rows.at[z], load_sem.at[0]),
        pltpu.make_async_copy(order_any, order, load_sem.at[0]),
    ]
    w_loads = [pltpu.make_async_copy(cross_w.at[0, l], weights.at[l], load_sem.at[1 + l]) for l in range(layers)]

    def send_block(q, chip, core):
        b, j = chunks[q]
        rank = ((chip // 2) * 2 + core) * CORES + j
        pltpu.make_async_remote_copy(
            src_ref=pooled.at[b, :, pl.ds(pl.multiple_of(rank * block, block), block)],
            dst_ref=arrived[q].at[r],
            send_sem=a2a_send.at[0],
            recv_sem=a2a_recv.at[q],
            device_id={"rank": chip * CORES + core},
            device_id_type=MESH,
        ).start()

    def send_rows(chip):
        for p in range(PIECES):
            pltpu.make_async_remote_copy(
                src_ref=mlp_w.at[pl.ds(p * piece, piece)],
                dst_ref=rows.at[z, pl.ds(p * piece, piece)],
                send_sem=row_send.at[0],
                recv_sem=row_recv.at[z, p],
                device_id={"rank": chip * CORES + c},
                device_id_type=MESH,
            ).start()

    def send_packs(chip):
        for i, ref in enumerate((hid_b, hid_o)):
            pltpu.make_async_remote_copy(
                src_ref=ref,
                dst_ref=packs.at[z, i],
                send_sem=pack_send.at[0],
                recv_sem=pack_recv.at[0],
                device_id={"rank": chip * CORES + c},
                device_id_type=MESH,
            ).start()

    @pl.when(outer)
    def _():
        pl.semaphore_wait(barrier, 2 * CORES)
        for q in range(len(chunks)):
            for chip in (there, here):
                for core in (c, 1 - c):
                    send_block(q, chip, core)
        for chip in (there, here):
            send_packs(chip)
        for chip in (there, here):
            send_rows(chip)

    width = block // n_tower

    def finish(count):
        drain(parts.at[:count], part_recv.at[0])
        logits = parts[0]
        for u in range(1, n_tower * CORES):
            logits = logits + parts[u]
        for u in range(n_tower):

            @pl.when(t == u)
            def _():
                for b in range(micro):
                    out[b] = logits[:, b * block + u * width : b * block + (u + 1) * width]

    @pl.when(inner)
    def _():
        for k in range(CORES):
            greet(rank=there * CORES + k)
        for k in range(CORES):
            greet(rank=3 * half * CORES + k)
            greet(rank=3 * (1 - half) * CORES + k)
        greet(rank=mate)
        for d in steps:
            greet(tower=t ^ d)
        for copy in own_loads + own_packs + loads + w_loads:
            copy.start()
        pl.semaphore_wait(barrier, 2 * CORES - 1 + len(steps))
        if len(steps) > 1:
            pl.semaphore_signal(diagonal, inc=1, device_id={"tower": t ^ 1}, device_id_type=MESH)
        for q in range(len(chunks)):
            for core in (c, 1 - c):
                send_block(q, there, core)
            send_block(q, here, 1 - c)
        send_packs(there)
        send_rows(there)

        for copy in loads:
            copy.wait()
        for l in range(layers):
            flat_v[l : l + 1, :] = bias_v[l]
        bias_c[...] = flat_v[...].T
        gain_c[...] = jnp.broadcast_to(gain_v[...], (8, CD)).T
        for q in range(len(chunks)):
            score[q] = jnp.zeros(score.shape[1:], jnp.float32)

        per_feature = n_rank // order.shape[1]
        height = arrived[0].shape[1]

        def tower(q):
            cols = slice(q * block, (q + 1) * block)
            drain(arrived[q], a2a_recv.at[q])
            for slot in range(order.shape[1]):
                feature = order[0, slot]
                for h in range(per_feature):
                    first[slot * E + h * height : slot * E + (h + 1) * height, cols] = arrived[q][
                        feature * per_feature + h
                    ]

            current, spare = first, state_a
            for l in range(layers):
                if q == 0:
                    w_loads[l].wait()
                for m in range(0, td, E):
                    at = slice(m, m + E)
                    product = (
                        jnp.dot(weights[l, at, :], current[:, cols], preferred_element_type=jnp.float32)
                        + bias_c[at, l : l + 1]
                    )
                    spare[at, cols] = (
                        first[at, cols].astype(jnp.float32) * product
                        + current[at, cols].astype(jnp.float32)
                    ).astype(jnp.bfloat16)
                current, spare = spare, (state_b if spare is state_a else state_a)
            squeezed = jnp.dot(compress_v[...], current[:, cols], preferred_element_type=jnp.float32)
            inverse_rms = lax.rsqrt(jnp.mean(squeezed * squeezed, axis=0, keepdims=True) + epsilon)
            towers[q][t] = (squeezed * inverse_rms * gain_c[:, 0:1]).astype(jnp.bfloat16)
            if q == 0 and len(steps) > 1:
                pl.semaphore_wait(diagonal, 1)
            for d in range(n_tower - 1, 0, -1):
                pltpu.make_async_remote_copy(
                    src_ref=towers[q].at[t],
                    dst_ref=towers[q].at[t],
                    send_sem=tower_send.at[0],
                    recv_sem=tower_recv.at[q],
                    device_id={"tower": t ^ d},
                    device_id_type=MESH,
                ).start()

        def mix(q):
            drain(towers[q].at[: n_tower - 1], tower_recv.at[q])
            values = [towers[q][u].astype(jnp.float32) for u in range(n_tower)]
            gram = {}
            for u in range(n_tower):
                for v in range(u, n_tower):
                    gram[u, v] = gram[v, u] = jnp.sum(values[u] * values[v], axis=0, keepdims=True) / CD
            for u in range(n_tower):
                total = values[u]
                for v in range(n_tower):
                    total = total + gram[u, v] * values[v]
                mixed[q][u * CD : (u + 1) * CD, :block] = total.astype(jnp.bfloat16)
            pltpu.make_async_remote_copy(
                src_ref=mixed[q].at[:, pl.ds(0, block)],
                dst_ref=mixed[q].at[:, pl.ds(block, block)],
                send_sem=mix_send.at[0],
                recv_sem=mix_recv.at[q],
                device_id={"rank": mate},
                device_id_type=MESH,
            ).start()

        def mate_mixed(q):
            drain(mixed[q].at[:, pl.ds(block, block)], mix_recv.at[q])

        def landed(s, p):
            drain(rows.at[s, pl.ds(p * piece, piece)], row_recv.at[s, p])

        def add(q, s, lo=0, hi=hid):
            hidden = jnp.dot(rows[s, lo:hi, :], mixed[q][...], preferred_element_type=jnp.float32)
            bias, weight = hid_c[s, 0, lo:hi, :], hid_c[s, 1, lo:hi, :]
            for k in range(CORES):
                at = slice(k * block, (k + 1) * block)
                terms = jnp.maximum(hidden[:, at] + bias, 0.0) * weight
                score[q, :, at] = score[q, :, at] + jnp.sum(terms.reshape(-1, 8, block), axis=0)

        def prepare():
            drain(packs, pack_recv.at[0])
            for s in range(packs.shape[0]):
                for i in range(2):
                    flat[2 * s + i : 2 * s + i + 1, :] = packs[s, i].astype(jnp.float32)
            turned = flat[...].T
            for s in range(packs.shape[0]):
                for i in range(2):
                    hid_c[s, i] = jnp.broadcast_to(turned[:, 2 * s + i : 2 * s + i + 1], (hid, block))

        far, near = 3 * (1 - half), 3 * half
        count = len(chunks)
        for q in range(count):
            tower(q)
            if q >= 2:
                mix(q - 2)
            if q == count - 1:
                prepare()
        mate_mixed(0)
        add(0, here)
        mix(count - 2)
        mate_mixed(1)
        add(1, here)
        mix(count - 1)
        for p in range(PIECES):
            landed(there, p)
        for p in range(PIECES):
            landed(far, p)
        for s in (there, far):
            for q in range(2):
                add(q, s)
        for q in range(2, count):
            mate_mixed(q)
            for s in (here, there, far):
                add(q, s)
        for p in range(PIECES):
            landed(near, p)
            for q in range(count):
                add(q, near, p * piece, (p + 1) * piece)

        me = t * CORES + c
        for q, (b, j) in enumerate(chunks):
            at = slice(b * block, (b + 1) * block)
            aside[c, j, :, at] = jnp.sum(score[q, :, :block], axis=0, keepdims=True)
            aside[1 - c, j, :, at] = jnp.sum(score[q, :, block:], axis=0, keepdims=True)
        for d in range(n_tower - 1, -1, -1):
            for k in (half, 1 - half):
                for j in range(CORES):
                    rank = (2 * half + k) * CORES + j

                    def hand_over(k=k, j=j, rank=rank, d=d):
                        pltpu.make_async_remote_copy(
                            src_ref=aside.at[k, j],
                            dst_ref=parts.at[me],
                            send_sem=part_send.at[0],
                            recv_sem=part_recv.at[0],
                            device_id={"tower": t ^ d, "rank": rank},
                            device_id_type=MESH,
                        ).start()

                    if d:
                        hand_over()
                    else:
                        pl.when(rank != r)(hand_over)
        parts[me] = aside[1 - half, c]

        for q in range(count):
            drain(arrived[q].at[:CORES + 1], a2a_send.at[0])
            drain(towers[q].at[: n_tower - 1], tower_send.at[0])
            drain(mixed[q].at[:, pl.ds(0, block)], mix_send.at[0])
        drain(packs.at[0], pack_send.at[0])
        drain(rows.at[0], row_send.at[0])
        finish(n_tower * CORES - 1)
        drain(parts, part_send.at[0])
        drain(parts.at[: n_tower * CORES - 1], part_send.at[0])

    @pl.when(outer)
    def _():
        for q in range(len(chunks)):
            drain(arrived[q].at[: 2 * CORES], a2a_send.at[0])
        drain(packs.at[:2], pack_send.at[0])
        drain(rows.at[:2], row_send.at[0])
        finish(n_tower * CORES)


def in_one_kernel(
    n_tower, n_rank, pooled, order, cross_w, cross_b, compress, gain, mlp_w, mlp_bias, out_weight
):
    micro, height, samples = pooled.shape
    block = samples // n_rank
    _, layers, td, _ = cross_w.shape
    hid, width = mlp_w.shape
    chips = n_rank // CORES
    count = micro * CORES
    every = count * block
    bf16, f32 = jnp.bfloat16, jnp.float32
    dma = pltpu.SemaphoreType.DMA
    hbm = pl.BlockSpec(memory_space=pl.ANY)
    return pl.pallas_call(
        functools.partial(fused, n_tower, n_rank),
        out_shape=pltpu.VMEM((micro, 1, block // n_tower), f32),
        in_specs=[hbm] * 9,
        out_specs=pl.BlockSpec(memory_space=pltpu.VMEM),
        scratch_shapes=[
            pltpu.SMEM(order.shape, order.dtype),
            [pltpu.VMEM((n_rank, height, block), bf16)] * count,
            pltpu.VMEM((layers, td, td), bf16),
            pltpu.VMEM((CD, td), bf16),
            pltpu.VMEM((layers, 1, td), f32),
            pltpu.VMEM((8, td), f32),
            pltpu.VMEM((1, CD), f32),
            pltpu.VMEM((td, 8), f32),
            pltpu.VMEM((CD, 8), f32),
            pltpu.VMEM((td, every), bf16),
            pltpu.VMEM((td, every), bf16),
            pltpu.VMEM((td, every), bf16),
            [pltpu.VMEM((n_tower, CD, block), bf16)] * count,
            [pltpu.VMEM((width, CORES * block), bf16)] * count,
            pltpu.VMEM((chips, hid, width), bf16),
            pltpu.VMEM((chips, 2, 1, hid), bf16),
            pltpu.VMEM((2 * chips, hid), f32),
            pltpu.VMEM((chips, 2, hid, block), f32),
            pltpu.VMEM((count, 8, CORES * block), f32),
            pltpu.VMEM((n_tower * CORES, 1, micro * block), f32),
            pltpu.VMEM((CORES, CORES, 1, micro * block), f32),
            pltpu.SemaphoreType.REGULAR,
            dma((1 + layers,)),
            dma((1,)),
            dma((count,)),
            dma((1,)),
            dma((chips, PIECES)),
            dma((1,)),
            dma((1,)),
            dma((1,)),
            dma((count,)),
            dma((1,)),
            dma((count,)),
            dma((1,)),
            dma((1,)),
        ],
        compiler_params=pltpu.CompilerParams(collective_id=0, has_side_effects=True),
    )(
        order,
        pooled,
        cross_w,
        cross_b.swapaxes(0, 1),
        compress,
        gain,
        mlp_w,
        mlp_bias[None],
        out_weight[None],
    )


def tower_block(first, weights, biases, compress, gain):
    first_f = first.astype(jnp.float32)
    current = first
    for layer in range(weights.shape[0]):
        product = (
            jnp.dot(weights[layer], current, preferred_element_type=jnp.float32)
            + biases[layer][:, None]
        )
        current = (first_f * product + current.astype(jnp.float32)).astype(jnp.bfloat16)
    squeezed = jnp.dot(compress, current, preferred_element_type=jnp.float32)
    inverse_rms = lax.rsqrt(jnp.mean(squeezed * squeezed, axis=0, keepdims=True) + epsilon)
    return (squeezed * inverse_rms * gain[:, None]).astype(jnp.bfloat16)


def interact(joined):
    samples_now = joined.shape[1]
    values_f = joined.astype(jnp.float32).reshape(-1, CD, samples_now)
    gram = jnp.einsum("tck,uck->tuk", values_f, values_f, precision=lax.Precision.HIGHEST) / CD
    mixed = values_f + jnp.einsum("tuk,uck->tck", gram, values_f, precision=lax.Precision.HIGHEST)
    return mixed.reshape(-1, samples_now).astype(jnp.bfloat16)


def logit_terms(hidden_rows, hidden_bias, hidden_out, features):
    hidden = (
        jnp.dot(hidden_rows, features, preferred_element_type=jnp.float32)
        + hidden_bias.astype(jnp.float32)[:, None]
    )
    return jnp.sum(
        jax.nn.relu(hidden) * hidden_out.astype(jnp.float32)[:, None], axis=0, keepdims=True
    )


def by_collectives(
    pooled,
    feature_order,
    cross_weight,
    cross_bias,
    compress_weight,
    norm_gain,
    mlp_weight,
    mlp_bias,
    out_weight,
):
    micro_count = pooled.shape[0]
    arriving = [
        lax.all_to_all(pooled[batch], "rank", split_axis=1, concat_axis=0, tiled=True)
        for batch in range(micro_count)
    ]
    hidden_rows, hidden_bias, hidden_out = (
        lax.all_gather(mlp_weight, "rank", axis=0, tiled=True),
        lax.all_gather(mlp_bias, "rank", axis=0, tiled=True),
        lax.all_gather(out_weight, "rank", axis=0, tiled=True),
    )
    results = []
    for batch in range(micro_count):
        arrived = arriving[batch]
        samples_here = arrived.shape[1]
        first = jnp.take(arrived.reshape(-1, E, samples_here), feature_order[0], axis=0).reshape(
            -1, samples_here
        )
        compressed = tower_block(
            first, cross_weight[0], cross_bias[0], compress_weight[0], norm_gain[0]
        )
        all_towers = lax.all_gather(compressed, "tower", axis=0, tiled=True)
        partial_value = logit_terms(hidden_rows, hidden_bias, hidden_out, interact(all_towers))
        logit_row = lax.psum_scatter(partial_value, "tower", scatter_dimension=1, tiled=True)
        results.append(logit_row)
    return jnp.stack(results)


def fits(mesh, pooled, mlp_w):
    towers, ranks = mesh.shape["tower"], mesh.shape["rank"]
    height, hid = pooled.shape[1], mlp_w.shape[0]
    return (
        ranks == LINE * CORES
        and towers in (1, 2, 4)
        and E % height == 0
        and height % 16 == 0
        and hid % 128 == 0
        and (pooled.shape[2] // ranks) % 128 == 0
    )


def solution(mesh):
    def on_device(*args):
        if fits(mesh, args[0], args[6]):
            return in_one_kernel(mesh.shape["tower"], mesh.shape["rank"], *args)
        return by_collectives(*args)

    return jax.shard_map(
        on_device,
        mesh=mesh,
        in_specs=(
            P(None, ("tower", "rank"), None),
            P("tower", None),
            P("tower", None, None, None),
            P("tower", None, None),
            P("tower", None, None),
            P("tower", None),
            P(("tower", "rank"), None),
            P(("tower", "rank")),
            P(("tower", "rank")),
        ),
        out_specs=P(None, "rank", "tower"),
        check_vma=False,
    )
```

time: 25.7 us -> 25.2 us (0.981)
  Pallas kernels: 25 us -> 24.5 us
    pallas_call x1, Pallas kernels: 25 us -> 24.5 us  [in_one_kernel(): pl.pallas_call(functools.partial(fused, n_tower, n_rank), out_shape=pltpu...]
where the time goes in v2:
time: 25.2 us; the launch traced here: 25.1 us
  Pallas kernels  24.5 us (97%)
  local copies, waits for them, and re-layouts  0.56 us (2%)
    pallas_call x1, Pallas kernels, in_one_kernel(): pl.pallas_call(functools.partial(fused, n_tower, n_rank), out_shape=pltpu...  24.5 us
    unnamed x1, local copies, waits for them, and re-layouts  0.56 us

profile of v2, /device:TPU:0, one launch (start us, length us, event | category | flops | bytes accessed | tf_op | source)
XLA Modules:
  0.0 25.1 jit_solution(14432284840591690947)
XLA Ops:
  0.0 24.5 %shard_map.91 = f32[2,1,32]{2,1,0:T(1,128)S(1)} custom-call(s32[1,4]{1,0:T(1,128)} %order_any.1, bf16[2,64,1024]{2,1,0:T(8,128)(2,1)} %pooled.1, bf16[1,3,512,512]{3,2,1,0:T(8,128)(2,1)} %cross_w.1, f32[3,1,512]{2,1,0:T(1,128)} %bitcast.3, bf16[1,128,512]{2,1,0:T(8,128)(2,1)} %compress.1, f32[1,128]{1,0:T(1,128)} %gain.1, bf16[128,512]{1,0:T(8,128)(2,1)} %mlp_w.1, ...), custom_call_target="tpu_custom_call" | custom-call | tf_op jit(solution)/shard_map/pallas_call | solution.py:380
  24.5 0.6 %copy.11 = f32[2,1,32]{2,1,0:T(1,128)} copy(f32[2,1,32]{2,1,0:T(1,128)S(1)} %shard_map.91) | data formatting | bytes 512

commit v3 on v2

--- a/solution.py
+++ b/solution.py
@@ -55,7 +55,7 @@
     score,
     parts,
     aside,
-    diagonal,
+    known,
     load_sem,
     a2a_send,
     a2a_recv,
@@ -83,6 +83,7 @@
     mate = z * CORES + (1 - c)
     half = z // 2
     here, there = 1 + half, 2 - half
+    near, far = 3 * half, 3 * (1 - half)
     inner = z == here
     outer = z != here
     steps = [1 << i for i in range(n_tower.bit_length() - 1)]
@@ -100,12 +101,12 @@
         )
         for q, (b, j) in enumerate(chunks)
     ]
-    own_packs = [pltpu.make_async_copy(ref, packs.at[z, i], pack_recv.at[0]) for i, ref in enumerate((hid_b, hid_o))]
+    own_packs = [pltpu.make_async_copy(ref, packs.at[half, z % 2, i], pack_recv.at[0]) for i, ref in enumerate((hid_b, hid_o))]
     loads = [
         pltpu.make_async_copy(cross_b, bias_v, load_sem.at[0]),
         pltpu.make_async_copy(gain, gain_v, load_sem.at[0]),
         pltpu.make_async_copy(compress.at[0], compress_v, load_sem.at[0]),
-        pltpu.make_async_copy(mlp_w, rows.at[z], load_sem.at[0]),
+        pltpu.make_async_copy(mlp_w, rows.at[half, pl.ds((z % 2) * hid, hid)], load_sem.at[0]),
         pltpu.make_async_copy(order_any, order, load_sem.at[0]),
     ]
     w_loads = [pltpu.make_async_copy(cross_w.at[0, l], weights.at[l], load_sem.at[1 + l]) for l in range(layers)]
@@ -126,7 +127,7 @@
         for p in range(PIECES):
             pltpu.make_async_remote_copy(
                 src_ref=mlp_w.at[pl.ds(p * piece, piece)],
-                dst_ref=rows.at[z, pl.ds(p * piece, piece)],
+                dst_ref=rows.at[half, pl.ds((z % 2) * hid + p * piece, piece)],
                 send_sem=row_send.at[0],
                 recv_sem=row_recv.at[z, p],
                 device_id={"rank": chip * CORES + c},
@@ -137,7 +138,7 @@
         for i, ref in enumerate((hid_b, hid_o)):
             pltpu.make_async_remote_copy(
                 src_ref=ref,
-                dst_ref=packs.at[z, i],
+                dst_ref=packs.at[half, z % 2, i],
                 send_sem=pack_send.at[0],
                 recv_sem=pack_recv.at[0],
                 device_id={"rank": chip * CORES + c},
@@ -151,9 +152,9 @@
             for chip in (there, here):
                 for core in (c, 1 - c):
                     send_block(q, chip, core)
-        for chip in (there, here):
+        for chip in (here, there):
             send_packs(chip)
-        for chip in (there, here):
+        for chip in (here, there):
             send_rows(chip)
 
     width = block // n_tower
@@ -175,8 +176,8 @@
         for k in range(CORES):
             greet(rank=there * CORES + k)
         for k in range(CORES):
-            greet(rank=3 * half * CORES + k)
-            greet(rank=3 * (1 - half) * CORES + k)
+            greet(rank=far * CORES + k)
+            greet(rank=near * CORES + k)
         greet(rank=mate)
         for d in steps:
             greet(tower=t ^ d)
@@ -184,7 +185,7 @@
             copy.start()
         pl.semaphore_wait(barrier, 2 * CORES - 1 + len(steps))
         if len(steps) > 1:
-            pl.semaphore_signal(diagonal, inc=1, device_id={"tower": t ^ 1}, device_id_type=MESH)
+            pl.semaphore_signal(known.at[0], inc=1, device_id={"tower": t ^ 1}, device_id_type=MESH)
         for q in range(len(chunks)):
             for core in (c, 1 - c):
                 send_block(q, there, core)
@@ -233,7 +234,7 @@
             inverse_rms = lax.rsqrt(jnp.mean(squeezed * squeezed, axis=0, keepdims=True) + epsilon)
             towers[q][t] = (squeezed * inverse_rms * gain_c[:, 0:1]).astype(jnp.bfloat16)
             if q == 0 and len(steps) > 1:
-                pl.semaphore_wait(diagonal, 1)
+                pl.semaphore_wait(known.at[0], 1)
             for d in range(n_tower - 1, 0, -1):
                 pltpu.make_async_remote_copy(
                     src_ref=towers[q].at[t],
@@ -269,11 +270,11 @@
             drain(mixed[q].at[:, pl.ds(block, block)], mix_recv.at[q])
 
         def landed(s, p):
-            drain(rows.at[s, pl.ds(p * piece, piece)], row_recv.at[s, p])
-
-        def add(q, s, lo=0, hi=hid):
-            hidden = jnp.dot(rows[s, lo:hi, :], mixed[q][...], preferred_element_type=jnp.float32)
-            bias, weight = hid_c[s, 0, lo:hi, :], hid_c[s, 1, lo:hi, :]
+            drain(rows.at[0, pl.ds(0, piece)], row_recv.at[s, p])
+
+        def add(q, pair):
+            hidden = jnp.dot(rows[pair], mixed[q][...], preferred_element_type=jnp.float32)
+            bias, weight = hid_c[pair, 0], hid_c[pair, 1]
             for k in range(CORES):
                 at = slice(k * block, (k + 1) * block)
                 terms = jnp.maximum(hidden[:, at] + bias, 0.0) * weight
@@ -281,43 +282,41 @@
 
         def prepare():
             drain(packs, pack_recv.at[0])
-            for s in range(packs.shape[0]):
+            for s in range(LINE):
                 for i in range(2):
-                    flat[2 * s + i : 2 * s + i + 1, :] = packs[s, i].astype(jnp.float32)
+                    flat[2 * s + i : 2 * s + i + 1, :] = packs[s // 2, s % 2, i].astype(jnp.float32)
             turned = flat[...].T
-            for s in range(packs.shape[0]):
+            for s in range(LINE):
                 for i in range(2):
-                    hid_c[s, i] = jnp.broadcast_to(turned[:, 2 * s + i : 2 * s + i + 1], (hid, block))
-
-        far, near = 3 * (1 - half), 3 * half
+                    hid_c[s // 2, i, (s % 2) * hid : (s % 2 + 1) * hid, :] = jnp.broadcast_to(
+                        turned[:, 2 * s + i : 2 * s + i + 1], (hid, block)
+                    )
+
         count = len(chunks)
-        for q in range(count):
-            tower(q)
-            if q >= 2:
-                mix(q - 2)
-            if q == count - 1:
-                prepare()
-        mate_mixed(0)
-        add(0, here)
-        mix(count - 2)
-        mate_mixed(1)
-        add(1, here)
-        mix(count - 1)
-        for p in range(PIECES):
-            landed(there, p)
-        for p in range(PIECES):
-            landed(far, p)
-        for s in (there, far):
-            for q in range(2):
-                add(q, s)
-        for q in range(2, count):
-            mate_mixed(q)
-            for s in (here, there, far):
-                add(q, s)
+        tower(0)
+        tower(1)
+        tower(2)
+        mix(0)
+        tower(3)
+        mix(1)
+        prepare()
+        mix(2)
         for p in range(PIECES):
             landed(near, p)
-            for q in range(count):
-                add(q, near, p * piece, (p + 1) * piece)
+        for q in range(2):
+            mate_mixed(q)
+            add(q, half)
+        mix(3)
+        mate_mixed(2)
+        add(2, half)
+        for s in (far, there):
+            for p in range(PIECES):
+                landed(s, p)
+        for q in range(3):
+            add(q, 1 - half)
+        mate_mixed(3)
+        add(3, half)
+        add(3, 1 - half)
 
         me = t * CORES + c
         for q, (b, j) in enumerate(chunks):
@@ -349,8 +348,8 @@
             drain(arrived[q].at[:CORES + 1], a2a_send.at[0])
             drain(towers[q].at[: n_tower - 1], tower_send.at[0])
             drain(mixed[q].at[:, pl.ds(0, block)], mix_send.at[0])
-        drain(packs.at[0], pack_send.at[0])
-        drain(rows.at[0], row_send.at[0])
+        drain(packs.at[0, 0], pack_send.at[0])
+        drain(rows.at[0, pl.ds(0, hid)], row_send.at[0])
         finish(n_tower * CORES - 1)
         drain(parts, part_send.at[0])
         drain(parts.at[: n_tower * CORES - 1], part_send.at[0])
@@ -359,8 +358,8 @@
     def _():
         for q in range(len(chunks)):
             drain(arrived[q].at[: 2 * CORES], a2a_send.at[0])
-        drain(packs.at[:2], pack_send.at[0])
-        drain(rows.at[:2], row_send.at[0])
+        drain(packs.at[0], pack_send.at[0])
+        drain(rows.at[0], row_send.at[0])
         finish(n_tower * CORES)
 
 
@@ -397,14 +396,14 @@
             pltpu.VMEM((td, every), bf16),
             [pltpu.VMEM((n_tower, CD, block), bf16)] * count,
             [pltpu.VMEM((width, CORES * block), bf16)] * count,
-            pltpu.VMEM((chips, hid, width), bf16),
-            pltpu.VMEM((chips, 2, 1, hid), bf16),
+            pltpu.VMEM((2, 2 * hid, width), bf16),
+            pltpu.VMEM((2, 2, 2, 1, hid), bf16),
             pltpu.VMEM((2 * chips, hid), f32),
-            pltpu.VMEM((chips, 2, hid, block), f32),
+            pltpu.VMEM((2, 2, 2 * hid, block), f32),
             pltpu.VMEM((count, 8, CORES * block), f32),
             pltpu.VMEM((n_tower * CORES, 1, micro * block), f32),
             pltpu.VMEM((CORES, CORES, 1, micro * block), f32),
-            pltpu.SemaphoreType.REGULAR,
+            pltpu.SemaphoreType.REGULAR((1,)),
             dma((1 + layers,)),
             dma((1,)),
             dma((count,)),
@@ -509,6 +508,7 @@
     return (
         ranks == LINE * CORES
         and towers in (1, 2, 4)
+        and pooled.shape[0] == 2
         and E % height == 0
         and height % 16 == 0
         and hid % 128 == 0

time: 25.2 us -> 24 us (0.952)
  Pallas kernels: 24.5 us -> 23.3 us
    pallas_call x1, Pallas kernels: 24.5 us -> 23.3 us  [in_one_kernel(): pl.pallas_call(functools.partial(fused, n_tower, n_rank), out_shape=pltpu...]
where the time goes in v3:
time: 24 us; the launch traced here: 23.9 us
  Pallas kernels  23.3 us (97%)
  local copies, waits for them, and re-layouts  0.56 us (2%)
    pallas_call x1, Pallas kernels, in_one_kernel(): pl.pallas_call(functools.partial(fused, n_tower, n_rank), out_shape=pltpu...  23.3 us
    unnamed x1, local copies, waits for them, and re-layouts  0.56 us

profile of v3, /device:TPU:0, one launch (start us, length us, event | category | flops | bytes accessed | tf_op | source)
XLA Modules:
  0.0 23.9 jit_solution(11529731122012391943)
XLA Ops:
  0.0 23.3 %shard_map.91 = f32[2,1,32]{2,1,0:T(1,128)S(1)} custom-call(s32[1,4]{1,0:T(1,128)} %order_any.1, bf16[2,64,1024]{2,1,0:T(8,128)(2,1)} %pooled.1, bf16[1,3,512,512]{3,2,1,0:T(8,128)(2,1)} %cross_w.1, f32[3,1,512]{2,1,0:T(1,128)} %bitcast.3, bf16[1,128,512]{2,1,0:T(8,128)(2,1)} %compress.1, f32[1,128]{1,0:T(1,128)} %gain.1, bf16[128,512]{1,0:T(8,128)(2,1)} %mlp_w.1, ...), custom_call_target="tpu_custom_call" | custom-call | tf_op jit(solution)/shard_map/pallas_call | solution.py:379
  23.3 0.6 %copy.11 = f32[2,1,32]{2,1,0:T(1,128)} copy(f32[2,1,32]{2,1,0:T(1,128)S(1)} %shard_map.91) | data formatting | bytes 512

commit v4 on v3

--- a/solution.py
+++ b/solution.py
@@ -11,7 +11,6 @@
 CD = 128
 CORES = 2
 LINE = 4
-PIECES = 2
 
 epsilon = 1e-06
 MESH = pl.DeviceIdType.MESH
@@ -74,7 +73,6 @@
     block = arrived[0].shape[-1]
     layers, td = cross_w.shape[1], cross_w.shape[2]
     hid = mlp_w.shape[0]
-    piece = hid // PIECES
     chunks = [(b, j) for b in range(micro) for j in range(CORES)]
     t = lax.axis_index("tower")
     r = lax.axis_index("rank")
@@ -123,16 +121,15 @@
             device_id_type=MESH,
         ).start()
 
-    def send_rows(chip):
-        for p in range(PIECES):
-            pltpu.make_async_remote_copy(
-                src_ref=mlp_w.at[pl.ds(p * piece, piece)],
-                dst_ref=rows.at[half, pl.ds((z % 2) * hid + p * piece, piece)],
-                send_sem=row_send.at[0],
-                recv_sem=row_recv.at[z, p],
-                device_id={"rank": chip * CORES + c},
-                device_id_type=MESH,
-            ).start()
+    def send_rows(chip, group):
+        pltpu.make_async_remote_copy(
+            src_ref=mlp_w,
+            dst_ref=rows.at[half, pl.ds((z % 2) * hid, hid)],
+            send_sem=row_send.at[0],
+            recv_sem=row_recv.at[group],
+            device_id={"rank": chip * CORES + c},
+            device_id_type=MESH,
+        ).start()
 
     def send_packs(chip):
         for i, ref in enumerate((hid_b, hid_o)):
@@ -148,14 +145,14 @@
     @pl.when(outer)
     def _():
         pl.semaphore_wait(barrier, 2 * CORES)
+        for chip in (there, here):
+            send_packs(chip)
         for q in range(len(chunks)):
             for chip in (there, here):
                 for core in (c, 1 - c):
                     send_block(q, chip, core)
-        for chip in (here, there):
-            send_packs(chip)
-        for chip in (here, there):
-            send_rows(chip)
+        send_rows(here, 0)
+        send_rows(there, 1)
 
     width = block // n_tower
 
@@ -186,12 +183,12 @@
         pl.semaphore_wait(barrier, 2 * CORES - 1 + len(steps))
         if len(steps) > 1:
             pl.semaphore_signal(known.at[0], inc=1, device_id={"tower": t ^ 1}, device_id_type=MESH)
+        send_packs(there)
         for q in range(len(chunks)):
             for core in (c, 1 - c):
                 send_block(q, there, core)
             send_block(q, here, 1 - c)
-        send_packs(there)
-        send_rows(there)
+        send_rows(there, 1)
 
         for copy in loads:
             copy.wait()
@@ -269,15 +266,13 @@
         def mate_mixed(q):
             drain(mixed[q].at[:, pl.ds(block, block)], mix_recv.at[q])
 
-        def landed(s, p):
-            drain(rows.at[0, pl.ds(0, piece)], row_recv.at[s, p])
-
-        def add(q, pair):
-            hidden = jnp.dot(rows[pair], mixed[q][...], preferred_element_type=jnp.float32)
+        def add(q, pair, sides=range(CORES)):
+            cols = slice(sides[0] * block, (sides[-1] + 1) * block)
+            hidden = jnp.dot(rows[pair], mixed[q][:, cols], preferred_element_type=jnp.float32)
             bias, weight = hid_c[pair, 0], hid_c[pair, 1]
-            for k in range(CORES):
+            for i, k in enumerate(sides):
                 at = slice(k * block, (k + 1) * block)
-                terms = jnp.maximum(hidden[:, at] + bias, 0.0) * weight
+                terms = jnp.maximum(hidden[:, i * block : (i + 1) * block] + bias, 0.0) * weight
                 score[q, :, at] = score[q, :, at] + jnp.sum(terms.reshape(-1, 8, block), axis=0)
 
         def prepare():
@@ -293,30 +288,27 @@
                     )
 
         count = len(chunks)
-        tower(0)
-        tower(1)
-        tower(2)
+        prepare()
+        for q in range(count):
+            tower(q)
         mix(0)
-        tower(3)
         mix(1)
-        prepare()
         mix(2)
-        for p in range(PIECES):
-            landed(near, p)
+        drain(rows.at[0, pl.ds(0, hid)], row_recv.at[0])
         for q in range(2):
             mate_mixed(q)
             add(q, half)
         mix(3)
         mate_mixed(2)
         add(2, half)
-        for s in (far, there):
-            for p in range(PIECES):
-                landed(s, p)
+        add(3, half, [0])
+        drain(rows.at[0], row_recv.at[1])
         for q in range(3):
             add(q, 1 - half)
+        add(3, 1 - half, [0])
         mate_mixed(3)
-        add(3, half)
-        add(3, 1 - half)
+        add(3, half, [1])
+        add(3, 1 - half, [1])
 
         me = t * CORES + c
         for q, (b, j) in enumerate(chunks):
@@ -408,7 +400,7 @@
             dma((1,)),
             dma((count,)),
             dma((1,)),
-            dma((chips, PIECES)),
+            dma((2,)),
             dma((1,)),
             dma((1,)),
             dma((1,)),

time: 24 us -> 23.6 us (0.983)
  Pallas kernels: 23.3 us -> 22.9 us
    pallas_call x1, Pallas kernels: 23.3 us -> 22.9 us  [in_one_kernel(): pl.pallas_call(functools.partial(fused, n_tower, n_rank), out_shape=pltpu...]
where the time goes in v4:
time: 23.6 us; the launch traced here: 23.5 us
  Pallas kernels  22.9 us (97%)
  local copies, waits for them, and re-layouts  0.56 us (2%)
    pallas_call x1, Pallas kernels, in_one_kernel(): pl.pallas_call(functools.partial(fused, n_tower, n_rank), out_shape=pltpu...  22.9 us
    unnamed x1, local copies, waits for them, and re-layouts  0.56 us

profile of v4, /device:TPU:0, one launch (start us, length us, event | category | flops | bytes accessed | tf_op | source)
XLA Modules:
  0.0 23.5 jit_solution(14583905941516234651)
XLA Ops:
  0.0 22.9 %shard_map.91 = f32[2,1,32]{2,1,0:T(1,128)S(1)} custom-call(s32[1,4]{1,0:T(1,128)} %order_any.1, bf16[2,64,1024]{2,1,0:T(8,128)(2,1)} %pooled.1, bf16[1,3,512,512]{3,2,1,0:T(8,128)(2,1)} %cross_w.1, f32[3,1,512]{2,1,0:T(1,128)} %bitcast.3, bf16[1,128,512]{2,1,0:T(8,128)(2,1)} %compress.1, f32[1,128]{1,0:T(1,128)} %gain.1, bf16[128,512]{1,0:T(8,128)(2,1)} %mlp_w.1, ...), custom_call_target="tpu_custom_call" | custom-call | tf_op jit(solution)/shard_map/pallas_call | solution.py:371
  23.0 0.6 %copy.11 = f32[2,1,32]{2,1,0:T(1,128)} copy(f32[2,1,32]{2,1,0:T(1,128)S(1)} %shard_map.91) | data formatting | bytes 512

commit v5 on v4

--- a/solution.py
+++ b/solution.py
@@ -107,7 +107,7 @@
         pltpu.make_async_copy(mlp_w, rows.at[half, pl.ds((z % 2) * hid, hid)], load_sem.at[0]),
         pltpu.make_async_copy(order_any, order, load_sem.at[0]),
     ]
-    w_loads = [pltpu.make_async_copy(cross_w.at[0, l], weights.at[l], load_sem.at[1 + l]) for l in range(layers)]
+    w_loads = [pltpu.make_async_copy(cross_w.at[0, l], weights.at[l], load_sem.at[1]) for l in range(layers)]
 
     def send_block(q, chip, core):
         b, j = chunks[q]
@@ -170,11 +170,9 @@
 
     @pl.when(inner)
     def _():
-        for k in range(CORES):
-            greet(rank=there * CORES + k)
-        for k in range(CORES):
-            greet(rank=far * CORES + k)
-            greet(rank=near * CORES + k)
+        for chip in (far, there, near):
+            for k in range(CORES):
+                greet(rank=chip * CORES + k)
         greet(rank=mate)
         for d in steps:
             greet(tower=t ^ d)
@@ -214,8 +212,9 @@
 
             current, spare = first, state_a
             for l in range(layers):
-                if q == 0:
-                    w_loads[l].wait()
+                if q == 0 and l == 0:
+                    for copy in w_loads:
+                        copy.wait()
                 for m in range(0, td, E):
                     at = slice(m, m + E)
                     product = (
@@ -254,14 +253,16 @@
                 for v in range(n_tower):
                     total = total + gram[u, v] * values[v]
                 mixed[q][u * CD : (u + 1) * CD, :block] = total.astype(jnp.bfloat16)
-            pltpu.make_async_remote_copy(
-                src_ref=mixed[q].at[:, pl.ds(0, block)],
-                dst_ref=mixed[q].at[:, pl.ds(block, block)],
-                send_sem=mix_send.at[0],
-                recv_sem=mix_recv.at[q],
-                device_id={"rank": mate},
-                device_id_type=MESH,
-            ).start()
+                if u % 2:
+                    part = pl.ds((u - 1) * CD, 2 * CD)
+                    pltpu.make_async_remote_copy(
+                        src_ref=mixed[q].at[part, pl.ds(0, block)],
+                        dst_ref=mixed[q].at[part, pl.ds(block, block)],
+                        send_sem=mix_send.at[0],
+                        recv_sem=mix_recv.at[q],
+                        device_id={"rank": mate},
+                        device_id_type=MESH,
+                    ).start()
 
         def mate_mixed(q):
             drain(mixed[q].at[:, pl.ds(block, block)], mix_recv.at[q])
@@ -286,6 +287,30 @@
                     hid_c[s // 2, i, (s % 2) * hid : (s % 2 + 1) * hid, :] = jnp.broadcast_to(
                         turned[:, 2 * s + i : 2 * s + i + 1], (hid, block)
                     )
+
+        me = t * CORES + c
+
+        def settle(side, j):
+            k = c if side == 0 else 1 - c
+            rank = (2 * half + k) * CORES + j
+            for b in range(micro):
+                at = slice(b * block, (b + 1) * block)
+                cols = slice(side * block, (side + 1) * block)
+                aside[k, j, :, at] = jnp.sum(score[b * CORES + j, :, cols], axis=0, keepdims=True)
+
+            def hand_over(d):
+                pltpu.make_async_remote_copy(
+                    src_ref=aside.at[k, j],
+                    dst_ref=parts.at[me],
+                    send_sem=part_send.at[0],
+                    recv_sem=part_recv.at[0],
+                    device_id={"tower": t ^ d, "rank": rank},
+                    device_id_type=MESH,
+                ).start()
+
+            for d in range(n_tower - 1, 0, -1):
+                hand_over(d)
+            pl.when(rank != r)(functools.partial(hand_over, 0))
 
         count = len(chunks)
         prepare()
@@ -306,34 +331,13 @@
         for q in range(3):
             add(q, 1 - half)
         add(3, 1 - half, [0])
+        for side, j in ((1, 0), (0, 0), (0, 1)):
+            settle(side, j)
         mate_mixed(3)
         add(3, half, [1])
         add(3, 1 - half, [1])
-
-        me = t * CORES + c
-        for q, (b, j) in enumerate(chunks):
-            at = slice(b * block, (b + 1) * block)
-            aside[c, j, :, at] = jnp.sum(score[q, :, :block], axis=0, keepdims=True)
-            aside[1 - c, j, :, at] = jnp.sum(score[q, :, block:], axis=0, keepdims=True)
-        for d in range(n_tower - 1, -1, -1):
-            for k in (half, 1 - half):
-                for j in range(CORES):
-                    rank = (2 * half + k) * CORES + j
-
-                    def hand_over(k=k, j=j, rank=rank, d=d):
-                        pltpu.make_async_remote_copy(
-                            src_ref=aside.at[k, j],
-                            dst_ref=parts.at[me],
-                            send_sem=part_send.at[0],
-                            recv_sem=part_recv.at[0],
-                            device_id={"tower": t ^ d, "rank": rank},
-                            device_id_type=MESH,
-                        ).start()
-
-                    if d:
-                        hand_over()
-                    else:
-                        pl.when(rank != r)(hand_over)
+        settle(1, 1)
+
         parts[me] = aside[1 - half, c]
 
         for q in range(count):
@@ -396,7 +400,7 @@
             pltpu.VMEM((n_tower * CORES, 1, micro * block), f32),
             pltpu.VMEM((CORES, CORES, 1, micro * block), f32),
             pltpu.SemaphoreType.REGULAR((1,)),
-            dma((1 + layers,)),
+            dma((2,)),
             dma((1,)),
             dma((count,)),
             dma((1,)),

time: 23.6 us -> 23.3 us (0.987)
    pallas_call x1, Pallas kernels: 22.9 us -> 22.7 us  [in_one_kernel(): pl.pallas_call(functools.partial(fused, n_tower, n_rank), out_shape=pltpu...]
where the time goes in v5:
time: 23.3 us; the launch traced here: 23.2 us
  Pallas kernels  22.7 us (97%)
  local copies, waits for them, and re-layouts  0.56 us (2%)
    pallas_call x1, Pallas kernels, in_one_kernel(): pl.pallas_call(functools.partial(fused, n_tower, n_rank), out_shape=pltpu...  22.7 us
    unnamed x1, local copies, waits for them, and re-layouts  0.56 us

profile of v5, /device:TPU:0, one launch (start us, length us, event | category | flops | bytes accessed | tf_op | source)
XLA Modules:
  0.0 23.2 jit_solution(6998171497826759882)
XLA Ops:
  0.0 22.7 %shard_map.91 = f32[2,1,32]{2,1,0:T(1,128)S(1)} custom-call(s32[1,4]{1,0:T(1,128)} %order_any.1, bf16[2,64,1024]{2,1,0:T(8,128)(2,1)} %pooled.1, bf16[1,3,512,512]{3,2,1,0:T(8,128)(2,1)} %cross_w.1, f32[3,1,512]{2,1,0:T(1,128)} %bitcast.3, bf16[1,128,512]{2,1,0:T(8,128)(2,1)} %compress.1, f32[1,128]{1,0:T(1,128)} %gain.1, bf16[128,512]{1,0:T(8,128)(2,1)} %mlp_w.1, ...), custom_call_target="tpu_custom_call" | custom-call | tf_op jit(solution)/shard_map/pallas_call | solution.py:375
  22.7 0.6 %copy.11 = f32[2,1,32]{2,1,0:T(1,128)} copy(f32[2,1,32]{2,1,0:T(1,128)S(1)} %shard_map.91) | data formatting | bytes 512

commit v6 on v5

--- a/solution.py
+++ b/solution.py
@@ -152,7 +152,7 @@
                 for core in (c, 1 - c):
                     send_block(q, chip, core)
         send_rows(here, 0)
-        send_rows(there, 1)
+        send_rows(there, 2)
 
     width = block // n_tower
 
@@ -276,6 +276,15 @@
                 terms = jnp.maximum(hidden[:, i * block : (i + 1) * block] + bias, 0.0) * weight
                 score[q, :, at] = score[q, :, at] + jnp.sum(terms.reshape(-1, 8, block), axis=0)
 
+        def add_one(q, chip):
+            here_rows = pl.ds(pl.multiple_of((chip % 2) * hid, hid), hid)
+            hidden = jnp.dot(rows[1 - half, here_rows, :], mixed[q][...], preferred_element_type=jnp.float32)
+            bias, weight = hid_c[1 - half, 0, here_rows, :], hid_c[1 - half, 1, here_rows, :]
+            for k in range(CORES):
+                at = slice(k * block, (k + 1) * block)
+                terms = jnp.maximum(hidden[:, at] + bias, 0.0) * weight
+                score[q, :, at] = score[q, :, at] + jnp.sum(terms.reshape(-1, 8, block), axis=0)
+
         def prepare():
             drain(packs, pack_recv.at[0])
             for s in range(LINE):
@@ -327,12 +336,17 @@
         mate_mixed(2)
         add(2, half)
         add(3, half, [0])
-        drain(rows.at[0], row_recv.at[1])
+        drain(rows.at[0, pl.ds(0, hid)], row_recv.at[1])
         for q in range(3):
-            add(q, 1 - half)
+            add_one(q, there)
+        drain(rows.at[0, pl.ds(0, hid)], row_recv.at[2])
+        add_one(0, far)
+        add_one(2, far)
+        settle(1, 0)
+        settle(0, 0)
+        add_one(1, far)
         add(3, 1 - half, [0])
-        for side, j in ((1, 0), (0, 0), (0, 1)):
-            settle(side, j)
+        settle(0, 1)
         mate_mixed(3)
         add(3, half, [1])
         add(3, 1 - half, [1])
@@ -404,7 +418,7 @@
             dma((1,)),
             dma((count,)),
             dma((1,)),
-            dma((2,)),
+            dma((3,)),
             dma((1,)),
             dma((1,)),
             dma((1,)),

time: 23.3 us -> 23.1 us (level)
  no operation moved by 1% of the time
where the time goes in v6:
time: 23.1 us; the launch traced here: 23 us
  Pallas kernels  22.5 us (97%)
  local copies, waits for them, and re-layouts  0.56 us (2%)
    pallas_call x1, Pallas kernels, in_one_kernel(): pl.pallas_call(functools.partial(fused, n_tower, n_rank), out_shape=pltpu...  22.5 us
    unnamed x1, local copies, waits for them, and re-layouts  0.56 us

profile of v6, /device:TPU:0, one launch (start us, length us, event | category | flops | bytes accessed | tf_op | source)
XLA Modules:
  0.0 23.0 jit_solution(6966174368214027418)
XLA Ops:
  0.0 22.5 %shard_map.91 = f32[2,1,32]{2,1,0:T(1,128)S(1)} custom-call(s32[1,4]{1,0:T(1,128)} %order_any.1, bf16[2,64,1024]{2,1,0:T(8,128)(2,1)} %pooled.1, bf16[1,3,512,512]{3,2,1,0:T(8,128)(2,1)} %cross_w.1, f32[3,1,512]{2,1,0:T(1,128)} %bitcast.3, bf16[1,128,512]{2,1,0:T(8,128)(2,1)} %compress.1, f32[1,128]{1,0:T(1,128)} %gain.1, bf16[128,512]{1,0:T(8,128)(2,1)} %mlp_w.1, ...), custom_call_target="tpu_custom_call" | custom-call | tf_op jit(solution)/shard_map/pallas_call | solution.py:389
  22.5 0.6 %copy.11 = f32[2,1,32]{2,1,0:T(1,128)} copy(f32[2,1,32]{2,1,0:T(1,128)S(1)} %shard_map.91) | data formatting | bytes 512

commit v7 on v6

--- a/solution.py
+++ b/solution.py
@@ -56,17 +56,12 @@
     aside,
     known,
     load_sem,
-    a2a_send,
+    sent,
     a2a_recv,
-    row_send,
     row_recv,
-    pack_send,
     pack_recv,
-    tower_send,
     tower_recv,
-    mix_send,
     mix_recv,
-    part_send,
     part_recv,
 ):
     micro = pooled.shape[0]
@@ -115,7 +110,7 @@
         pltpu.make_async_remote_copy(
             src_ref=pooled.at[b, :, pl.ds(pl.multiple_of(rank * block, block), block)],
             dst_ref=arrived[q].at[r],
-            send_sem=a2a_send.at[0],
+            send_sem=sent.at[0],
             recv_sem=a2a_recv.at[q],
             device_id={"rank": chip * CORES + core},
             device_id_type=MESH,
@@ -125,7 +120,7 @@
         pltpu.make_async_remote_copy(
             src_ref=mlp_w,
             dst_ref=rows.at[half, pl.ds((z % 2) * hid, hid)],
-            send_sem=row_send.at[0],
+            send_sem=sent.at[0],
             recv_sem=row_recv.at[group],
             device_id={"rank": chip * CORES + c},
             device_id_type=MESH,
@@ -136,7 +131,7 @@
             pltpu.make_async_remote_copy(
                 src_ref=ref,
                 dst_ref=packs.at[half, z % 2, i],
-                send_sem=pack_send.at[0],
+                send_sem=sent.at[0],
                 recv_sem=pack_recv.at[0],
                 device_id={"rank": chip * CORES + c},
                 device_id_type=MESH,
@@ -235,7 +230,7 @@
                 pltpu.make_async_remote_copy(
                     src_ref=towers[q].at[t],
                     dst_ref=towers[q].at[t],
-                    send_sem=tower_send.at[0],
+                    send_sem=sent.at[0],
                     recv_sem=tower_recv.at[q],
                     device_id={"tower": t ^ d},
                     device_id_type=MESH,
@@ -258,7 +253,7 @@
                     pltpu.make_async_remote_copy(
                         src_ref=mixed[q].at[part, pl.ds(0, block)],
                         dst_ref=mixed[q].at[part, pl.ds(block, block)],
-                        send_sem=mix_send.at[0],
+                        send_sem=sent.at[0],
                         recv_sem=mix_recv.at[q],
                         device_id={"rank": mate},
                         device_id_type=MESH,
@@ -311,7 +306,7 @@
                 pltpu.make_async_remote_copy(
                     src_ref=aside.at[k, j],
                     dst_ref=parts.at[me],
-                    send_sem=part_send.at[0],
+                    send_sem=sent.at[0],
                     recv_sem=part_recv.at[0],
                     device_id={"tower": t ^ d, "rank": rank},
                     device_id_type=MESH,
@@ -332,13 +327,13 @@
         for q in range(2):
             mate_mixed(q)
             add(q, half)
-        mix(3)
         mate_mixed(2)
         add(2, half)
-        add(3, half, [0])
         drain(rows.at[0, pl.ds(0, hid)], row_recv.at[1])
         for q in range(3):
             add_one(q, there)
+        mix(3)
+        add(3, half, [0])
         drain(rows.at[0, pl.ds(0, hid)], row_recv.at[2])
         add_one(0, far)
         add_one(2, far)
@@ -355,21 +350,21 @@
         parts[me] = aside[1 - half, c]
 
         for q in range(count):
-            drain(arrived[q].at[:CORES + 1], a2a_send.at[0])
-            drain(towers[q].at[: n_tower - 1], tower_send.at[0])
-            drain(mixed[q].at[:, pl.ds(0, block)], mix_send.at[0])
-        drain(packs.at[0, 0], pack_send.at[0])
-        drain(rows.at[0, pl.ds(0, hid)], row_send.at[0])
+            drain(arrived[q].at[:CORES + 1], sent.at[0])
+            drain(towers[q].at[: n_tower - 1], sent.at[0])
+            drain(mixed[q].at[:, pl.ds(0, block)], sent.at[0])
+        drain(packs.at[0, 0], sent.at[0])
+        drain(rows.at[0, pl.ds(0, hid)], sent.at[0])
         finish(n_tower * CORES - 1)
-        drain(parts, part_send.at[0])
-        drain(parts.at[: n_tower * CORES - 1], part_send.at[0])
+        drain(parts, sent.at[0])
+        drain(parts.at[: n_tower * CORES - 1], sent.at[0])
 
     @pl.when(outer)
     def _():
         for q in range(len(chunks)):
-            drain(arrived[q].at[: 2 * CORES], a2a_send.at[0])
-        drain(packs.at[0], pack_send.at[0])
-        drain(rows.at[0], row_send.at[0])
+            drain(arrived[q].at[: 2 * CORES], sent.at[0])
+        drain(packs.at[0], sent.at[0])
+        drain(rows.at[0], sent.at[0])
         finish(n_tower * CORES)
 
 
@@ -417,15 +412,10 @@
             dma((2,)),
             dma((1,)),
             dma((count,)),
-            dma((1,)),
             dma((3,)),
             dma((1,)),
-            dma((1,)),
-            dma((1,)),
             dma((count,)),
-            dma((1,)),
             dma((count,)),
-            dma((1,)),
             dma((1,)),
         ],
         compiler_params=pltpu.CompilerParams(collective_id=0, has_side_effects=True),

time: 23.1 us -> 23.1 us (level)
  no operation moved by 1% of the time
where the time goes in v7:
time: 23.1 us; the launch traced here: 23 us
  Pallas kernels  22.4 us (97%)
  local copies, waits for them, and re-layouts  0.56 us (2%)
    pallas_call x1, Pallas kernels, in_one_kernel(): pl.pallas_call(functools.partial(fused, n_tower, n_rank), out_shape=pltpu...  22.4 us
    unnamed x1, local copies, waits for them, and re-layouts  0.56 us

profile of v7, /device:TPU:0, one launch (start us, length us, event | category | flops | bytes accessed | tf_op | source)
XLA Modules:
  0.0 23.0 jit_solution(6253448819624857145)
XLA Ops:
  0.0 22.4 %shard_map.91 = f32[2,1,32]{2,1,0:T(1,128)S(1)} custom-call(s32[1,4]{1,0:T(1,128)} %order_any.1, bf16[2,64,1024]{2,1,0:T(8,128)(2,1)} %pooled.1, bf16[1,3,512,512]{3,2,1,0:T(8,128)(2,1)} %cross_w.1, f32[3,1,512]{2,1,0:T(1,128)} %bitcast.3, bf16[1,128,512]{2,1,0:T(8,128)(2,1)} %compress.1, f32[1,128]{1,0:T(1,128)} %gain.1, bf16[128,512]{1,0:T(8,128)(2,1)} %mlp_w.1, ...), custom_call_target="tpu_custom_call" | custom-call | tf_op jit(solution)/shard_map/pallas_call | solution.py:384
  22.4 0.6 %copy.11 = f32[2,1,32]{2,1,0:T(1,128)} copy(f32[2,1,32]{2,1,0:T(1,128)S(1)} %shard_map.91) | data formatting | bytes 512
